TPU v7x, 256 devices: a whole 4x4x8 slice. The times are simulated.
256 devices in a mesh: seq: 32 (over y, x, core), exp: 8 (over z).
Axes of the slice: x: 4, y: 4, z: 8, core: 2. Of those that a mesh axis runs over, the one named last changes fastest.
Arguments:
- mixer_input: bfloat16 [4096, 8192], P('seq', 'exp'), may hold values from -6 to 6
- gate_input: bfloat16 [4096, 8192], P('seq', 'exp'), may hold values from -6 to 6
- delta_raw: bfloat16 [4096, 8192], P('seq', 'exp'), may hold values from -7 to 16387
- input_coef: bfloat16 [4096, 16], P('seq'), may hold values from 0.19921875 to 1.796875
- output_coef: bfloat16 [4096, 16], P('seq'), may hold values from -3 to 3
- decay_rate: float32 [16, 8192], P(None, 'exp'), may hold values from 4.8828125e-06 to 0.05
- conv_weight: float32 [4, 8192], P(None, 'exp'), may hold values from -3 to 3
- conv_bias: float32 [8192], P('exp'), may hold values from -3 to 3
- skip_gain: float32 [8192], P('exp'), may hold values from 0.5 to 1.5
- out_weight: bfloat16 [8192, 4096], P('exp', 'seq'), may hold values from -0.0625 to 0.0625
- residual: bfloat16 [4096, 4096], P(('seq', 'exp')), may hold values from -6 to 6
- norm_gain: float32 [4096], replicated, may hold values from 0.1 to 1.9
- router_weight: bfloat16 [4096, 8], replicated, may hold values from -0.09375 to 0.09375
- expert_ids: int32 [4096, 2], P(('seq', 'exp')), may hold values from 0 to 7, all different within a row; in each aligned block of 16 rows (0 to 15, 16 to 31, ...) at most 5 rows name the same one
- gate_weight: bfloat16 [8, 4096, 12288], P('exp', None, 'seq'), may hold values from -0.09375 to 0.09375
- up_weight: bfloat16 [8, 4096, 12288], P('exp', None, 'seq'), may hold values from -0.09375 to 0.09375
- down_weight: bfloat16 [8, 12288, 4096], P('exp', 'seq'), may hold values from -0.0546875 to 0.0546875
Outputs:
- mixed: bfloat16 [4096, 8192], P('seq', 'exp')
- final: bfloat16 [4096, 4096], P(('seq', 'exp'))
Inputs may be any that keep to these rules, and one draw needn't show every extreme that they name: `expert_ids`: each row names two different experts. In each aligned block of 16 rows (the rows of one device) no expert is named by more than 5 rows, and in some block one expert is named by exactly 5 rows.
All inputs are finite; a program needn't handle non-finite values.
Results may differ from a plain program's by a relative error of at most 0.015.
Values may be sent and summed in bfloat16 or wider, within the bound.
No kernel may reach another device: no remote copies, remote signals or barrier semaphores. Data moves between devices by JAX's collectives and lax.ppermute only.
A program may use at most 128 MiB of HBM per device.

v0:
```python
import jax
import jax.numpy as jnp
from jax import lax
from jax.sharding import PartitionSpec as P

KCONV = 4


def from_behind(block, axis, distance):
    devices = range(lax.axis_size(axis))
    route = [(i - distance, i) for i in devices if i - distance in devices]
    return lax.ppermute(block, axis, route)


def carried_in(part, axis, combine, identity):
    place = lax.axis_index(axis)
    gathered = jax.tree.map(lambda a: lax.all_gather(a, axis), part)
    state = jax.tree.map(lambda a, e: jnp.zeros_like(a) + jnp.asarray(e, a.dtype), part, identity)

    def one(turn, state):
        return combine(
            state, jax.tree.map(lambda a: lax.dynamic_index_in_dim(a, turn, 0, False), gathered)
        )

    return lax.fori_loop(0, place, one, state)


def sweep(state, delta, convolved, input_rows, output_rows, decay_rate):

    def advance(carry, inputs):
        delta_row, value_row, input_row, output_row = inputs
        retain = jnp.exp(-delta_row[None, :] * decay_rate)
        carry = retain * carry + (1.0 - retain) * input_row[:, None] * value_row[None, :]
        return (carry, jnp.sum(output_row[:, None] * carry, axis=0))

    return lax.scan(advance, state, (delta, convolved, input_rows, output_rows), unroll=8)


def chain(earlier, later):
    return (earlier[0] * later[0], later[0] * earlier[1] + later[1])


def shards(
    mixer_input,
    gate_input,
    delta_raw,
    input_coef,
    output_coef,
    decay_rate,
    conv_weight,
    conv_bias,
    skip_gain,
    out_weight,
    residual,
    norm_gain,
    router_weight,
    expert_ids,
    gate_weight,
    up_weight,
    down_weight,
):
    length = mixer_input.shape[0]
    width = mixer_input.shape[1]
    tail = mixer_input[length - (KCONV - 1) :]
    before = from_behind(tail, "seq", 1)
    padded = jnp.concatenate([before, mixer_input], axis=0).astype(jnp.float32)
    summed = jnp.broadcast_to(conv_bias[None, :], (length, width))
    for offset in range(KCONV):
        summed = summed + conv_weight[offset][None, :] * padded[offset : offset + length]
    convolved = jax.nn.silu(summed)
    delta = jax.nn.softplus(delta_raw.astype(jnp.float32))
    input_rows = input_coef.astype(jnp.float32)
    output_rows = output_coef.astype(jnp.float32)
    zero_state = jnp.zeros(decay_rate.shape, jnp.float32)
    end_state, local_out = sweep(zero_state, delta, convolved, input_rows, output_rows, decay_rate)
    block_decay = jnp.exp(-jnp.sum(delta, axis=0)[None, :] * decay_rate)
    carried_decay, start_state = carried_in(
        (block_decay, end_state), "seq", chain, (jnp.ones_like(block_decay), zero_state)
    )
    last_state, scan_out = sweep(start_state, delta, convolved, input_rows, output_rows, decay_rate)
    mixed = (
        (scan_out + skip_gain[None, :] * convolved) * jax.nn.silu(gate_input.astype(jnp.float32))
    ).astype(jnp.bfloat16)
    rows = residual.shape[0]
    model_width = residual.shape[1]
    full_weight = lax.all_gather(out_weight, "seq", axis=1, tiled=True)
    projected = lax.psum_scatter(
        jnp.dot(mixed, full_weight, preferred_element_type=jnp.float32).astype(jnp.bfloat16),
        "exp",
        scatter_dimension=0,
        tiled=True,
    ).astype(jnp.float32)
    hidden_state = residual.astype(jnp.float32) + projected
    scale = lax.rsqrt(jnp.mean(hidden_state * hidden_state, axis=1, keepdims=True) + 1e-06)
    normed = (hidden_state * scale * norm_gain[None, :]).astype(jnp.bfloat16)
    experts = router_weight.shape[1]
    capacity = 2 * rows // experts + 1
    logits = jnp.dot(normed, router_weight, preferred_element_type=jnp.float32)
    expert_range = jnp.arange(experts, dtype=jnp.int32)
    matches = expert_ids[:, :, None] == expert_range[None, None, :]
    chosen = jnp.sum(jnp.where(matches, logits[:, None, :], 0.0), axis=2)
    first = jax.nn.sigmoid(chosen[:, 0] - chosen[:, 1])
    flat_ids = expert_ids.reshape(-1)
    position = jnp.arange(flat_ids.shape[0], dtype=jnp.int32)
    earlier = (flat_ids[:, None] == flat_ids[None, :]) & (position[None, :] < position[:, None])
    rank = jnp.sum(earlier.astype(jnp.int32), axis=1)
    target = flat_ids * capacity + rank
    placing = (jnp.arange(experts * capacity, dtype=jnp.int32)[:, None] == target[None, :]).astype(
        jnp.bfloat16
    )
    repeated = jnp.broadcast_to(normed[:, None, :], (rows, 2, model_width)).reshape(-1, model_width)
    outgoing = (
        jnp.dot(placing, repeated, preferred_element_type=jnp.float32)
        .astype(jnp.bfloat16)
        .reshape(experts, capacity, model_width)
    )
    arrived = lax.all_to_all(outgoing, "exp", split_axis=0, concat_axis=0, tiled=True)
    flat_rows = arrived.reshape(-1, arrived.shape[2])
    piece = lax.all_gather(flat_rows, "seq", axis=0, tiled=True)
    gating = jnp.dot(piece, gate_weight[0], preferred_element_type=jnp.float32)
    upward = jnp.dot(piece, up_weight[0], preferred_element_type=jnp.float32)
    activated = (jax.nn.silu(gating) * upward).astype(jnp.bfloat16)
    partial_out = jnp.dot(activated, down_weight[0], preferred_element_type=jnp.float32)
    summed_out = lax.psum_scatter(
        partial_out.astype(jnp.bfloat16), "seq", scatter_dimension=0, tiled=True
    )
    returned = lax.all_to_all(
        summed_out.reshape(arrived.shape), "exp", split_axis=0, concat_axis=0, tiled=True
    )
    flat_returned = returned.reshape(-1, model_width)
    picked = jnp.einsum(
        "sa,sd->ad", placing, flat_returned, preferred_element_type=jnp.float32
    ).reshape(rows, 2, model_width)
    moe_out = first[:, None] * picked[:, 0] + (1.0 - first)[:, None] * picked[:, 1]
    final = (hidden_state + moe_out).astype(jnp.bfloat16)
    return (mixed, final)


def solution(mesh):
    return jax.shard_map(
        shards,
        mesh=mesh,
        in_specs=(
            P("seq", "exp"),
            P("seq", "exp"),
            P("seq", "exp"),
            P("seq", None),
            P("seq", None),
            P(None, "exp"),
            P(None, "exp"),
            P("exp"),
            P("exp"),
            P("exp", "seq"),
            P(("seq", "exp"), None),
            P(),
            P(),
            P(("seq", "exp"), None),
            P("exp", None, "seq"),
            P("exp", None, "seq"),
            P("exp", "seq", None),
        ),
        out_specs=(P("seq", "exp"), P(("seq", "exp"), None)),
        check_vma=False,
    )
```

profile of v0, /device:TPU:2, one launch (start us, length us, event | category | flops | bytes accessed | tf_op | source)
XLA Modules:
  0.0 486.0 jit_solution(3095711971764541297)
XLA Ops:
  8.1 2.0 collective-permute-start
  10.2 2.1 fusion.59
  12.2 1.5 multiply_exponential_fusion
  13.8 0.9 fusion.71
  15.5 1.0 maximum_convert_fusion
  17.3 1.8 fusion.81
  19.2 24.8 %while.37 = (s32[]{:T(128)}, f32[16,1024]{1,0:T(8,128)S(1)}, f32[16,8,1024]{2,1,0:T(8,128)}, f32[16,1024]{1,0:T(8,128)S(1)}, f32[16,8,16]{2,1,0:T(8,128)S(1)}, /...) while((s32[]{:T(128)}, f32[16,1024]{1,0:T(8,128)S(1)}, ...), condition=%wide.region_2.3_spmd.clone, body=%wide.region_1.2_spmd.clone.sunk | while | flops 811018 | bytes 396055 | solution.py:36
  19.2 1.3 constant_dynamic-slice_fusion.41
  20.7 1.3 constant_dynamic-slice_fusion.41
  22.3 1.4 constant_dynamic-slice_fusion.41
  23.9 1.3 constant_dynamic-slice_fusion.41
  25.4 1.3 constant_dynamic-slice_fusion.41
  26.9 1.3 constant_dynamic-slice_fusion.41
  28.5 1.3 constant_dynamic-slice_fusion.41
  30.0 1.5 constant_dynamic-slice_fusion.41
  31.8 1.3 constant_dynamic-slice_fusion.41
  33.3 1.3 constant_dynamic-slice_fusion.41
  34.8 1.3 constant_dynamic-slice_fusion.41
  36.4 1.3 constant_dynamic-slice_fusion.41
  37.9 1.3 constant_dynamic-slice_fusion.41
  39.5 1.3 constant_dynamic-slice_fusion.41
  41.0 1.3 constant_dynamic-slice_fusion.41
  42.5 1.3 constant_dynamic-slice_fusion.41
  45.6 20.6 %all-gather.11.cloned.1.call-done = f32[512,1024]{1,0:T(8,128)} async-done(((f32[16,1024]{1,0:T(8,128)}), f32[512,1024]{1,0:T(8,128)}) %all-gather.11.cloned.1.call-update) | async-done | bytes 2097168 | tf_op jit(solution)/shard_map/all_gather | solution.py:17
  66.2 51.3 %all-gather.13.cloned.1.call-done = f32[512,1024]{1,0:T(8,128)} async-done(((f32[16,1024]{1,0:T(8,128)}), f32[512,1024]{1,0:T(8,128)}) %all-gather.13.cloned.1.call-update) | async-done | bytes 2097168 | tf_op jit(solution)/shard_map/all_gather | solution.py:17
  117.5 1.8 while.35
  117.5 0.9 bitcast_add_fusion.3
  118.4 0.9 bitcast_add_fusion.3
  119.4 40.2 %while.36 = (s32[]{:T(128)}, f32[16,1024]{1,0:T(8,128)S(1)}, f32[16,8,1024]{2,1,0:T(8,128)}, f32[16,8,1024]{2,1,0:T(8,128)}, f32[16,1024]{1,0:T(8,128)S(1)}, /*i...) while((s32[]{:T(128)}, f32[16,1024]{1,0:T(8,128)S(1)}, ...), condition=%wide.region_14.15_spmd, body=%wide.region_5.14_spmd.sunk | while | flops 1441801 | bytes 1316385 | solution.py:36
  119.4 1.3 constant_dynamic-slice_fusion.40
  121.9 1.3 constant_dynamic-slice_fusion.40
  124.4 1.4 constant_dynamic-slice_fusion.40
  127.0 1.3 constant_dynamic-slice_fusion.40
  129.5 1.3 constant_dynamic-slice_fusion.40
  132.0 1.3 constant_dynamic-slice_fusion.40
  134.4 1.3 constant_dynamic-slice_fusion.40
  136.9 1.5 constant_dynamic-slice_fusion.40
  139.6 1.3 constant_dynamic-slice_fusion.40
  142.1 1.3 constant_dynamic-slice_fusion.40
  144.6 1.3 constant_dynamic-slice_fusion.40
  147.2 1.3 constant_dynamic-slice_fusion.40
  149.7 1.3 constant_dynamic-slice_fusion.40
  152.2 1.3 constant_dynamic-slice_fusion.40
  154.7 1.3 constant_dynamic-slice_fusion.40
  157.1 1.3 constant_dynamic-slice_fusion.40
  159.6 2.5 fusion.58
  162.2 21.8 %all-gather.7.cloned.1.call-done = bf16[1024,4096]{1,0:T(8,128)(2,1)} async-done(((bf16[1024,128]{1,0:T(8,128)(2,1)}), bf16[1024,4096]{1,0:T(8,128)(2,1)}) %all-gather.7.cloned.1.call-update) | async-done | bytes 8388624 | tf_op jit(solution)/shard_map/all_gather | solution.py:86
  184.0 5.7 %convolution_convert_fusion.1 = bf16[128,4096]{1,0:T(8,128)(2,1)} fusion(bf16[128,1024]{1,0:T(8,128)(2,1)S(1)} %fusion.58, bf16[1024,4096]{1,0:T(8,128)(2,1)} %all-gather.7.cloned.1.call-done), kind=kOutput, calls=%fused_computation.111 | convolution fusion | flops 1074266112 | bytes 9699328 | tf_op jit(solution)/shard_map/dot_general | solution.py:88
  191.4 41.3 %reduce-scatter.3.cloned.1.call-done = bf16[16,4096]{1,0:T(8,128)(2,1)} async-done(((bf16[128,4096]{1,0:T(8,128)(2,1)}), bf16[16,4096]{1,0:T(8,128)(2,1)}) %reduce-scatter.3.cloned.1.call-update) | async-done | bytes 131088 | tf_op jit(solution)/shard_map/reduce_scatter | solution.py:87
  232.7 1.1 multiply_reduce_fusion.8
  233.8 1.0 multiply_convert_fusion
  236.4 1.2 convolution_convert_fusion.2
  237.6 0.9 reshape.357
  238.6 18.0 %all_to_all.10 = bf16[8,5,4096]{2,1,0:T(8,128)(2,1)} all-to-all(bf16[8,5,4096]{2,1,0:T(8,128)(2,1)} %reshape.357), channel_id=1, replica_groups=mesh['seq'=32,'exp'=8] {'exp'}, dimensions={0} | all-to-all | bytes 655360 | tf_op jit(solution)/shard_map/all_to_all | solution.py:117
  256.5 1.9 reshape.358
  258.5 59.5 %all-gather.9.cloned.1.call-done = bf16[1280,4096]{1,0:T(8,128)(2,1)} async-done(((bf16[40,4096]{1,0:T(8,128)(2,1)}), bf16[1280,4096]{1,0:T(8,128)(2,1)}) %all-gather.9.cloned.1.call-update) | async-done | bytes 10485776 | tf_op jit(solution)/shard_map/all_gather | solution.py:119
  318.0 10.2 %fusion.33 = f32[1280,384]{1,0:T(8,128)} fusion(bf16[1280,4096]{1,0:T(8,128)(2,1)} %all-gather.9.cloned.1.call-done, bf16[1,4096,384]{2,1,0:T(8,128)(2,1)} %param.37), kind=kOutput, calls=%fused_computation.116 | convolution fusion | flops 4026531840 | bytes 15597568 | tf_op jit(solution)/shard_map/dot_general | solution.py:120
  328.2 17.2 %convolution_convert_fusion = bf16[1280,4096]{1,0:T(8,128)(2,1)} fusion(bf16[1,384,4096]{2,1,0:T(8,128)(2,1)S(1)} %copy-done, bf16[1280,4096]{1,0:T(8,128)(2,1)} %all-gather.9.cloned.1.call-done, bf16[1,4096,384]{2,1,0:T(8,128)(2,1)} %param.38, f32[1280,384]{1,0:T(8,128)} %fusion.33), kind=kOutput, calls=%fused_computation.110 | convolution fusion | flops 8061255680 | bytes 29229056 | tf_op jit(solution)/shard_map/dot_general | solution.py:123
  345.4 105.2 %reduce-scatter.5.cloned.1.call-done = bf16[40,4096]{1,0:T(8,128)(2,1)} async-done(((bf16[1280,4096]{1,0:T(8,128)(2,1)}), bf16[40,4096]{1,0:T(8,128)(2,1)}) %reduce-scatter.5.cloned.1.call-update) | async-done | bytes 327696 | tf_op jit(solution)/shard_map/reduce_scatter | solution.py:124
  450.6 1.9 reshape.359
  452.5 7.0 %all-to-all-start.1 = ((bf16[8,5,4096]{2,1,0:T(8,128)(2,1)}), bf16[8,5,4096]{2,1,0:T(8,128)(2,1)}, u32[]{:S(2)}, u32[]{:S(2)}) async-start(bf16[8,5,4096]{2,1,0:T(8,128)(2,1)} %reshape.359), calls=%async_computation.3 | async-start | bytes 1048576 | tf_op jit(solution)/shard_map/all_to_all | solution.py:127
  459.9 16.1 %all-to-all-done.1 = bf16[8,5,4096]{2,1,0:T(8,128)(2,1)} async-done(((bf16[8,5,4096]{2,1,0:T(8,128)(2,1)}), bf16[8,5,4096]{2,1,0:T(8,128)(2,1)}, u32[]{:S(2)}, u32[]{:S(2)}) %all-to-all-start.1) | async-done | bytes 327712 | tf_op jit(solution)/shard_map/all_to_all | solution.py:127
  476.0 1.2 reshape.367
  477.4 1.7 fusion.64
  (255 shorter events, 29.4 us)
Async XLA Ops:
  7.2 321.0 %copy-start = (bf16[1,384,4096]{2,1,0:T(8,128)(2,1)S(1)}, bf16[1,384,4096]{2,1,0:T(8,128)(2,1)}, u32[]{:S(2)}) copy-start(bf16[1,384,4096]{2,1,0:T(8,128)(2,1)} %param.39) | copy-start | bytes 9437188
  7.2 12.0 %copy-start.2 = (f32[16,1024]{1,0:T(8,128)S(1)}, f32[16,1024]{1,0:T(8,128)}, u32[]{:S(2)}) copy-start(f32[16,1024]{1,0:T(8,128)} %param.28) | copy-start | bytes 196612
  7.2 59.0 %all-gather.11.cloned.1.call-start = ((), (), s32[]{:S(2)}) async-start(), calls=%async_computation.8 | async-start | bytes 2162688 | tf_op jit(solution)/shard_map/all_gather | solution.py:17
  8.1 7.4 %collective-permute-start = (bf16[3,1024]{1,0:T(4,128)(2,1)S(1)}, bf16[3,1024]{1,0:T(4,128)(2,1)S(1)}, u32[]{:S(2)}, u32[]{:S(2)}) collective-permute-start(bf16[3,1024]{1,0:T(4,128)(2,1)S(1)} %slice.264), channel_id=1, source_target_pairs={{0,8},{8,16},{16,24},{24,32},{32,40},{40,48},{48,56},{56,64},{64,7... | collective-permute-start | bytes 18440 | tf_op jit(solution)/shard_map/ppermute | solution.py:12
  13.8 103.8 %all-gather.13.cloned.1.call-start = ((), (), s32[]{:S(2)}) async-start(), calls=%async_computation.9 | async-start | bytes 2162688 | tf_op jit(solution)/shard_map/all_gather | solution.py:17
  16.5 0.8 copy-start.1
  16.5 29.0 %copy-start.12 = (bf16[128,16]{0,1:T(8,128)(2,1)S(1)}, bf16[128,16]{0,1:T(8,128)(2,1)}, u32[]{:S(2)}) copy-start(bf16[128,16]{0,1:T(8,128)(2,1)} %param.27) | copy-start | bytes 12292
  44.0 0.6 copy-start.3
  44.7 139.3 %all-gather.7.cloned.1.call-start = ((), (), s32[]{:S(2)}) async-start(), calls=%async_computation.4 | async-start | bytes 8650752 | tf_op jit(solution)/shard_map/all_gather | solution.py:86
  45.4 187.3 %reduce-scatter.3.cloned.1.call-start = ((), (), s32[]{:S(2)}) async-start(), calls=%async_computation.5 | async-start | bytes 1179648 | tf_op jit(solution)/shard_map/reduce_scatter | solution.py:87
  119.3 40.3 %copy-start.9 = (f32[1024]{0:T(1024)S(1)}, f32[1024]{0:T(1024)}, u32[]{:S(2)}) copy-start(f32[1024]{0:T(1024)} %param.30) | copy-start | bytes 12292
  119.4 40.3 %copy-start.11 = (f32[1024]{0:T(1024)S(1)}, f32[1024]{0:T(1024)}, u32[]{:S(2)}) copy-start(f32[1024]{0:T(1024)} %param.31) | copy-start | bytes 12292
  162.2 27.5 %copy-start.4 = (bf16[128,1024]{1,0:T(8,128)(2,1)}, bf16[128,1024]{1,0:T(8,128)(2,1)S(1)}, u32[]{:S(2)}) copy-start(bf16[128,1024]{1,0:T(8,128)(2,1)S(1)} %fusion.58) | copy-start | bytes 786436
  162.2 70.5 %copy-start.7 = (bf16[16,4096]{1,0:T(8,128)(2,1)S(1)}, bf16[16,4096]{1,0:T(8,128)(2,1)}, u32[]{:S(2)}) copy-start(bf16[16,4096]{1,0:T(8,128)(2,1)} %param.33) | copy-start | bytes 393220
  162.2 71.6 %copy-start.10 = (f32[4096]{0:T(1024)S(1)}, f32[4096]{0:T(1024)}, u32[]{:S(2)}) copy-start(f32[4096]{0:T(1024)} %param.34) | copy-start | bytes 49156
  189.7 128.3 %all-gather.9.cloned.1.call-start = ((), (), s32[]{:S(2)}) async-start(), calls=%async_computation.6 | async-start | bytes 10813440 | tf_op jit(solution)/shard_map/all_gather | solution.py:119
  234.8 0.7 copy-start.5
  258.5 192.2 %reduce-scatter.5.cloned.1.call-start = ((), (), s32[]{:S(2)}) async-start(), calls=%async_computation.7 | async-start | bytes 10813440 | tf_op jit(solution)/shard_map/reduce_scatter | solution.py:124
  345.4 114.2 %copy-start.14 = (s32[32]{0:T(128)S(1)}, s32[32]{0:T(128)}, u32[]{:S(2)}) copy-start(s32[32]{0:T(128)} %multiply_add_fusion.8) | copy-start | bytes 388
  345.4 114.3 %copy-start.6 = (bf16[16,4096]{1,0:T(8,128)(2,1)S(1)}, bf16[16,4096]{1,0:T(8,128)(2,1)}, u32[]{:S(2)}) copy-start(bf16[16,4096]{1,0:T(8,128)(2,1)} %copy-done.5) | copy-start | bytes 393220
  345.4 114.3 %copy-start.8 = (bf16[4096,8]{0,1:T(8,128)(2,1)S(1)}, bf16[4096,8]{0,1:T(8,128)(2,1)}, u32[]{:S(2)}) copy-start(bf16[4096,8]{0,1:T(8,128)(2,1)} %param.35) | copy-start | bytes 196612
  345.4 114.4 %copy-start.13 = (s32[16,2]{0,1:T(2,128)S(1)}, s32[16,2]{0,1:T(2,128)}, u32[]{:S(2)}) copy-start(s32[16,2]{0,1:T(2,128)} %param.36) | copy-start | bytes 388
  452.5 23.4 %all-to-all-start.1 = ((bf16[8,5,4096]{2,1,0:T(8,128)(2,1)}), bf16[8,5,4096]{2,1,0:T(8,128)(2,1)}, u32[]{:S(2)}, u32[]{:S(2)}) async-start(bf16[8,5,4096]{2,1,0:T(8,128)(2,1)} %reshape.359), calls=%async_computation.3 | async-start | bytes 1048576 | tf_op jit(solution)/shard_map/all_to_all | solution.py:127
Sparse Core Ops, SparseCore 0:
  13.9 52.2 all-gather.10
  69.3 48.1 all-gather.12
  120.0 63.9 all-gather.6
  189.8 42.8 reduce-scatter.2
  258.6 59.3 all-gather.8
  345.5 105.0 reduce-scatter.4
where the time goes:
time: 492 us; the launch traced here: 486 us
  waiting for transfers between devices  317 us (64%)
  other arithmetic  67.9 us (14%)
  matrix products  34.6 us (7%)
  local copies, waits for them, and re-layouts  24 us (5%)
  blocking collectives  18 us (4%)
  between operations  14.4 us (3%)
  starting transfers between devices  9.3 us (2%)
    reduce_scatter x1, waiting for transfers between devices, shards(): lax.psum_scatter(partial_out.astype(jnp.bfloat16), 'seq', scatter_dimensi...  105 us
    all_gather x2, waiting for transfers between devices, carried_in(): gathered = jax.tree.map(lambda a: lax.all_gather(a, axis), part)  71.9 us
    all_gather x1, waiting for transfers between devices, shards(): piece = lax.all_gather(flat_rows, 'seq', axis=0, tiled=True)  59.5 us
    slice x32, other arithmetic, sweep(): lax.scan(advance, state, (delta, convolved, input_rows, output_rows), unr...  42.6 us
    reduce_scatter x1, waiting for transfers between devices, shards(): lax.psum_scatter(jnp.dot(mixed, full_weight, preferred_element_type=jnp.f...  41.3 us
    all_gather x1, waiting for transfers between devices, shards(): full_weight = lax.all_gather(out_weight, 'seq', axis=1, tiled=True)  21.8 us
    all_to_all x1, blocking collectives, shards(): lax.all_to_all(outgoing, 'exp', split_axis=0, concat_axis=0, tiled=True)  18 us
    dot_general x1, matrix products, shards(): jnp.dot(activated, down_weight[0], preferred_element_type=jnp.float32)  17.2 us
  transfers between devices with their start and end apart: 8, of which 7 were waited for; matrix products, arithmetic and copies ran while one was open for 16% of the time, Pallas kernels for 0%

commit v1 on v0

--- a/solution.py
+++ b/solution.py
@@ -83,7 +83,9 @@
     ).astype(jnp.bfloat16)
     rows = residual.shape[0]
     model_width = residual.shape[1]
-    full_weight = lax.all_gather(out_weight, "seq", axis=1, tiled=True)
+    full_weight = jnp.concatenate(
+        lax.all_to_all(jnp.stack([out_weight] * lax.axis_size("seq")), "seq", 0, 0), axis=1
+    )
     projected = lax.psum_scatter(
         jnp.dot(mixed, full_weight, preferred_element_type=jnp.float32).astype(jnp.bfloat16),
         "exp",

time: 492 us -> 545 us (1.11)
  waiting for transfers between devices: 317 us -> 355 us
  starting transfers between devices: 9.3 us -> 18.1 us
    all_gather x2, waiting for transfers between devices: 71.9 us -> 110 us  [carried_in(): gathered = jax.tree.map(lambda a: lax.all_gather(a, axis), part)]
    reduce_scatter x1, waiting for transfers between devices: 41.3 us -> 64.1 us  [shards(): lax.psum_scatter(jnp.dot(mixed, full_weight, preferred_element_type=jnp.f...]
    all_gather x1 -> x0, waiting for transfers between devices: 21.8 us -> none  [shards(): full_weight = lax.all_gather(out_weight, 'seq', axis=1, tiled=True)]
    all_to_all x0 -> x1, starting transfers between devices: none -> 8.71 us  [shards(): lax.all_to_all(jnp.stack([out_weight] * lax.axis_size('seq')), 'seq', 0, 0)]
  transfers between devices with their start and end apart: 8 -> 8, of which waited for: 7 -> 6; matrix products, arithmetic and copies ran while one was open for 16% -> 15% of each run, Pallas kernels for 0% -> 0%
where the time goes in v1:
time: 545 us; the launch traced here: 539 us
  waiting for transfers between devices  355 us (65%)
  other arithmetic  67.3 us (12%)
  matrix products  36.4 us (7%)
  local copies, waits for them, and re-layouts  29.3 us (5%)
  starting transfers between devices  18.1 us (3%)
  blocking collectives  18 us (3%)
  between operations  14 us (3%)
    all_gather x2, waiting for transfers between devices, carried_in(): gathered = jax.tree.map(lambda a: lax.all_gather(a, axis), part)  110 us
    reduce_scatter x1, waiting for transfers between devices, shards(): lax.psum_scatter(partial_out.astype(jnp.bfloat16), 'seq', scatter_dimensi...  105 us
    reduce_scatter x1, waiting for transfers between devices, shards(): lax.psum_scatter(jnp.dot(mixed, full_weight, preferred_element_type=jnp.f...  64.1 us
    all_gather x1, waiting for transfers between devices, shards(): piece = lax.all_gather(flat_rows, 'seq', axis=0, tiled=True)  59.3 us
    slice x32, other arithmetic, sweep(): lax.scan(advance, state, (delta, convolved, input_rows, output_rows), unr...  42.6 us
    all_to_all x1, blocking collectives, shards(): lax.all_to_all(outgoing, 'exp', split_axis=0, concat_axis=0, tiled=True)  18 us
    dot_general x1, matrix products, shards(): jnp.dot(activated, down_weight[0], preferred_element_type=jnp.float32)  17.2 us
    all_to_all x1, waiting for transfers between devices, shards(): lax.all_to_all(summed_out.reshape(arrived.shape), 'exp', split_axis=0, co...  16.1 us
  transfers between devices with their start and end apart: 8, of which 6 were waited for; matrix products, arithmetic and copies ran while one was open for 15% of the time, Pallas kernels for 0%

profile of v1, /device:TPU:2, one launch (start us, length us, event | category | flops | bytes accessed | tf_op | source)
XLA Modules:
  0.0 539.2 jit_solution(2513918077394352957)
XLA Ops:
  8.1 2.0 collective-permute-start
  10.2 2.1 fusion.59
  12.2 1.5 multiply_exponential_fusion
  15.5 1.0 maximum_convert_fusion
  17.3 1.8 fusion.81
  19.2 24.9 %while.37 = (s32[]{:T(128)}, f32[16,1024]{1,0:T(8,128)S(1)}, f32[16,8,1024]{2,1,0:T(8,128)}, f32[16,1024]{1,0:T(8,128)S(1)}, f32[16,8,16]{2,1,0:T(8,128)S(1)}, /...) while((s32[]{:T(128)}, f32[16,1024]{1,0:T(8,128)S(1)}, ...), condition=%wide.region_2.3_spmd.clone, body=%wide.region_1.2_spmd.clone.sunk | while | flops 811018 | bytes 396055 | solution.py:36
  19.2 1.3 constant_dynamic-slice_fusion.41
  20.7 1.3 constant_dynamic-slice_fusion.41
  22.2 1.3 constant_dynamic-slice_fusion.41
  23.8 1.3 constant_dynamic-slice_fusion.41
  25.3 1.3 constant_dynamic-slice_fusion.41
  26.8 1.4 constant_dynamic-slice_fusion.41
  28.5 1.3 constant_dynamic-slice_fusion.41
  30.0 1.3 constant_dynamic-slice_fusion.41
  31.5 1.3 constant_dynamic-slice_fusion.41
  33.0 1.5 constant_dynamic-slice_fusion.41
  34.8 1.3 constant_dynamic-slice_fusion.41
  36.4 1.3 constant_dynamic-slice_fusion.41
  37.9 1.3 constant_dynamic-slice_fusion.41
  39.4 1.3 constant_dynamic-slice_fusion.41
  41.0 1.4 constant_dynamic-slice_fusion.41
  42.6 1.3 constant_dynamic-slice_fusion.41
  44.7 1.1 copy.33
  45.8 4.3 stack.2
  50.1 8.7 %all-to-all-start = ((bf16[32,1024,128]{1,2,0:T(8,128)(2,1)}), bf16[32,1024,128]{1,2,0:T(8,128)(2,1)}, u32[]{:S(2)}, u32[]{:S(2)}) async-start(bf16[32,1024,128]{1,2,0:T(8,128)(2,1)} %stack.2), calls=%async_computation | async-start | bytes 16777216 | tf_op jit(solution)/shard_map/all_to_all | solution.py:87
  59.0 9.3 %all-gather.8.cloned.1.call-done = f32[512,1024]{1,0:T(8,128)} async-done(((f32[16,1024]{1,0:T(8,128)}), f32[512,1024]{1,0:T(8,128)}) %all-gather.8.cloned.1.call-update) | async-done | bytes 2097168 | tf_op jit(solution)/shard_map/all_gather | solution.py:17
  68.3 100.7 %all-gather.10.cloned.1.call-done = f32[512,1024]{1,0:T(8,128)} async-done(((f32[16,1024]{1,0:T(8,128)}), f32[512,1024]{1,0:T(8,128)}) %all-gather.10.cloned.1.call-update) | async-done | bytes 2097168 | tf_op jit(solution)/shard_map/all_gather | solution.py:17
  169.0 1.8 while.35
  169.9 0.9 bitcast_add_fusion.3
  170.8 40.3 %while.36 = (s32[]{:T(128)}, f32[16,1024]{1,0:T(8,128)S(1)}, f32[16,8,1024]{2,1,0:T(8,128)}, f32[16,8,1024]{2,1,0:T(8,128)}, f32[16,1024]{1,0:T(8,128)S(1)}, /*i...) while((s32[]{:T(128)}, f32[16,1024]{1,0:T(8,128)S(1)}, ...), condition=%wide.region_14.15_spmd, body=%wide.region_5.14_spmd.sunk | while | flops 1441801 | bytes 1316385 | solution.py:36
  170.9 1.3 constant_dynamic-slice_fusion.40
  173.4 1.3 constant_dynamic-slice_fusion.40
  175.9 1.3 constant_dynamic-slice_fusion.40
  178.4 1.3 constant_dynamic-slice_fusion.40
  180.9 1.3 constant_dynamic-slice_fusion.40
  183.4 1.4 constant_dynamic-slice_fusion.40
  185.9 1.3 constant_dynamic-slice_fusion.40
  188.4 1.3 constant_dynamic-slice_fusion.40
  190.9 1.3 constant_dynamic-slice_fusion.40
  193.4 1.5 constant_dynamic-slice_fusion.40
  196.1 1.3 constant_dynamic-slice_fusion.40
  198.6 1.3 constant_dynamic-slice_fusion.40
  201.1 1.3 constant_dynamic-slice_fusion.40
  203.6 1.3 constant_dynamic-slice_fusion.40
  206.1 1.4 constant_dynamic-slice_fusion.40
  208.7 1.3 constant_dynamic-slice_fusion.40
  211.1 2.4 fusion.58
  213.6 7.4 %convolution_convert_fusion.1 = bf16[128,4096]{1,0:T(8,128)(2,1)} fusion(bf16[128,1024]{1,0:T(8,128)(2,1)S(1)} %fusion.58, bf16[1024,4096]{0,1:T(8,128)(2,1)} %bitcast.55), kind=kOutput, calls=%fused_computation.111 | convolution fusion | flops 1074266112 | bytes 9699328 | tf_op jit(solution)/shard_map/dot_general | solution.py:90
  222.2 64.1 %reduce-scatter.3.cloned.1.call-done = bf16[16,4096]{1,0:T(8,128)(2,1)} async-done(((bf16[128,4096]{1,0:T(8,128)(2,1)}), bf16[16,4096]{1,0:T(8,128)(2,1)}) %reduce-scatter.3.cloned.1.call-update) | async-done | bytes 131088 | tf_op jit(solution)/shard_map/reduce_scatter | solution.py:89
  286.3 1.1 multiply_reduce_fusion.8
  287.4 1.0 multiply_convert_fusion
  290.0 1.2 convolution_convert_fusion.2
  291.2 0.9 reshape.367
  292.1 18.0 %all_to_all.15 = bf16[8,5,4096]{2,1,0:T(8,128)(2,1)} all-to-all(bf16[8,5,4096]{2,1,0:T(8,128)(2,1)} %reshape.367), channel_id=1, replica_groups=mesh['seq'=32,'exp'=8] {'exp'}, dimensions={0} | all-to-all | bytes 655360 | tf_op jit(solution)/shard_map/all_to_all | solution.py:119
  310.1 1.9 reshape.368
  312.3 59.3 %all-gather.6.cloned.1.call-done = bf16[1280,4096]{1,0:T(8,128)(2,1)} async-done(((bf16[40,4096]{1,0:T(8,128)(2,1)}), bf16[1280,4096]{1,0:T(8,128)(2,1)}) %all-gather.6.cloned.1.call-update) | async-done | bytes 10485776 | tf_op jit(solution)/shard_map/all_gather | solution.py:121
  371.6 10.2 %fusion.33 = f32[1280,384]{1,0:T(8,128)} fusion(bf16[1280,4096]{1,0:T(8,128)(2,1)} %all-gather.6.cloned.1.call-done, bf16[1,4096,384]{2,1,0:T(8,128)(2,1)} %param.37), kind=kOutput, calls=%fused_computation.116 | convolution fusion | flops 4026531840 | bytes 15597568 | tf_op jit(solution)/shard_map/dot_general | solution.py:122
  381.8 17.2 %convolution_convert_fusion = bf16[1280,4096]{1,0:T(8,128)(2,1)} fusion(bf16[1,384,4096]{2,1,0:T(8,128)(2,1)S(1)} %copy-done, bf16[1280,4096]{1,0:T(8,128)(2,1)} %all-gather.6.cloned.1.call-done, bf16[1,4096,384]{2,1,0:T(8,128)(2,1)} %param.38, f32[1280,384]{1,0:T(8,128)} %fusion.33), kind=kOutput, calls=%fused_computation.110 | convolution fusion | flops 8061255680 | bytes 29229056 | tf_op jit(solution)/shard_map/dot_general | solution.py:125
  399.0 105.2 %reduce-scatter.5.cloned.1.call-done = bf16[40,4096]{1,0:T(8,128)(2,1)} async-done(((bf16[1280,4096]{1,0:T(8,128)(2,1)}), bf16[40,4096]{1,0:T(8,128)(2,1)}) %reduce-scatter.5.cloned.1.call-update) | async-done | bytes 327696 | tf_op jit(solution)/shard_map/reduce_scatter | solution.py:126
  504.2 1.9 reshape.369
  506.1 7.0 %all-to-all-start.2 = ((bf16[8,5,4096]{2,1,0:T(8,128)(2,1)}), bf16[8,5,4096]{2,1,0:T(8,128)(2,1)}, u32[]{:S(2)}, u32[]{:S(2)}) async-start(bf16[8,5,4096]{2,1,0:T(8,128)(2,1)} %reshape.369), calls=%async_computation.4 | async-start | bytes 1048576 | tf_op jit(solution)/shard_map/all_to_all | solution.py:129
  513.5 16.1 %all-to-all-done.2 = bf16[8,5,4096]{2,1,0:T(8,128)(2,1)} async-done(((bf16[8,5,4096]{2,1,0:T(8,128)(2,1)}), bf16[8,5,4096]{2,1,0:T(8,128)(2,1)}, u32[]{:S(2)}, u32[]{:S(2)}) %all-to-all-start.2) | async-done | bytes 327712 | tf_op jit(solution)/shard_map/all_to_all | solution.py:129
  529.6 1.2 reshape.377
  531.0 1.7 fusion.64
  (250 shorter events, 30.1 us)
Async XLA Ops:
  7.2 374.6 %copy-start = (bf16[1,384,4096]{2,1,0:T(8,128)(2,1)S(1)}, bf16[1,384,4096]{2,1,0:T(8,128)(2,1)}, u32[]{:S(2)}) copy-start(bf16[1,384,4096]{2,1,0:T(8,128)(2,1)} %param.39) | copy-start | bytes 9437188
  7.2 12.0 %copy-start.2 = (f32[16,1024]{1,0:T(8,128)S(1)}, f32[16,1024]{1,0:T(8,128)}, u32[]{:S(2)}) copy-start(f32[16,1024]{1,0:T(8,128)} %param.28) | copy-start | bytes 196612
  7.2 61.1 %all-gather.8.cloned.1.call-start = ((), (), s32[]{:S(2)}) async-start(), calls=%async_computation.8 | async-start | bytes 2162688 | tf_op jit(solution)/shard_map/all_gather | solution.py:17
  8.1 7.4 %collective-permute-start = (bf16[3,1024]{1,0:T(4,128)(2,1)S(1)}, bf16[3,1024]{1,0:T(4,128)(2,1)S(1)}, u32[]{:S(2)}, u32[]{:S(2)}) collective-permute-start(bf16[3,1024]{1,0:T(4,128)(2,1)S(1)} %slice.264), channel_id=1, source_target_pairs={{0,8},{8,16},{16,24},{24,32},{32,40},{40,48},{48,56},{56,64},{64,7... | collective-permute-start | bytes 18440 | tf_op jit(solution)/shard_map/ppermute | solution.py:12
  13.7 155.3 %all-gather.10.cloned.1.call-start = ((), (), s32[]{:S(2)}) async-start(), calls=%async_computation.9 | async-start | bytes 2162688 | tf_op jit(solution)/shard_map/all_gather | solution.py:17
  16.5 0.8 copy-start.1
  44.0 0.6 copy-start.3
  50.1 8.8 %copy-start.10 = (bf16[128,16]{0,1:T(8,128)(2,1)S(1)}, bf16[128,16]{0,1:T(8,128)(2,1)}, u32[]{:S(2)}) copy-start(bf16[128,16]{0,1:T(8,128)(2,1)} %param.27) | copy-start | bytes 12292
  50.1 163.5 %all-to-all-start = ((bf16[32,1024,128]{1,2,0:T(8,128)(2,1)}), bf16[32,1024,128]{1,2,0:T(8,128)(2,1)}, u32[]{:S(2)}, u32[]{:S(2)}) async-start(bf16[32,1024,128]{1,2,0:T(8,128)(2,1)} %stack.2), calls=%async_computation | async-start | bytes 16777216 | tf_op jit(solution)/shard_map/all_to_all | solution.py:87
  58.8 227.5 %reduce-scatter.3.cloned.1.call-start = ((), (), s32[]{:S(2)}) async-start(), calls=%async_computation.5 | async-start | bytes 1179648 | tf_op jit(solution)/shard_map/reduce_scatter | solution.py:89
  213.5 7.5 %copy-start.7 = (bf16[128,1024]{1,0:T(8,128)(2,1)}, bf16[128,1024]{1,0:T(8,128)(2,1)S(1)}, u32[]{:S(2)}) copy-start(bf16[128,1024]{1,0:T(8,128)(2,1)S(1)} %fusion.58) | copy-start | bytes 786436
  213.6 72.7 %copy-start.6 = (bf16[16,4096]{1,0:T(8,128)(2,1)S(1)}, bf16[16,4096]{1,0:T(8,128)(2,1)}, u32[]{:S(2)}) copy-start(bf16[16,4096]{1,0:T(8,128)(2,1)} %param.33) | copy-start | bytes 393220
  213.6 73.8 %copy-start.9 = (f32[4096]{0:T(1024)S(1)}, f32[4096]{0:T(1024)}, u32[]{:S(2)}) copy-start(f32[4096]{0:T(1024)} %param.34) | copy-start | bytes 49156
  221.1 150.5 %all-gather.6.cloned.1.call-start = ((), (), s32[]{:S(2)}) async-start(), calls=%async_computation.6 | async-start | bytes 10813440 | tf_op jit(solution)/shard_map/all_gather | solution.py:121
  288.4 0.7 copy-start.4
  312.1 192.2 %reduce-scatter.5.cloned.1.call-start = ((), (), s32[]{:S(2)}) async-start(), calls=%async_computation.7 | async-start | bytes 10813440 | tf_op jit(solution)/shard_map/reduce_scatter | solution.py:126
  399.0 114.3 %copy-start.5 = (bf16[16,4096]{1,0:T(8,128)(2,1)S(1)}, bf16[16,4096]{1,0:T(8,128)(2,1)}, u32[]{:S(2)}) copy-start(bf16[16,4096]{1,0:T(8,128)(2,1)} %copy-done.4) | copy-start | bytes 393220
  399.0 114.3 %copy-start.8 = (bf16[4096,8]{0,1:T(8,128)(2,1)S(1)}, bf16[4096,8]{0,1:T(8,128)(2,1)}, u32[]{:S(2)}) copy-start(bf16[4096,8]{0,1:T(8,128)(2,1)} %param.35) | copy-start | bytes 196612
  399.0 114.4 %copy-start.11 = (s32[16,2]{0,1:T(2,128)S(1)}, s32[16,2]{0,1:T(2,128)}, u32[]{:S(2)}) copy-start(s32[16,2]{0,1:T(2,128)} %param.36) | copy-start | bytes 388
  506.1 23.4 %all-to-all-start.2 = ((bf16[8,5,4096]{2,1,0:T(8,128)(2,1)}), bf16[8,5,4096]{2,1,0:T(8,128)(2,1)}, u32[]{:S(2)}, u32[]{:S(2)}) async-start(bf16[8,5,4096]{2,1,0:T(8,128)(2,1)} %reshape.369), calls=%async_computation.4 | async-start | bytes 1048576 | tf_op jit(solution)/shard_map/all_to_all | solution.py:129
Sparse Core Ops, SparseCore 0:
  13.9 54.4 all-gather.7
  71.4 97.5 all-gather.9
  221.2 65.0 reduce-scatter.2
  312.2 59.3 all-gather.5
  399.1 105.0 reduce-scatter.4
